TPU v7x, 512 devices: a whole 4x8x8 slice. The times are simulated.
512 devices in a mesh: gx: 32 (over y, x), gy: 16 (over z, core).
Axes of the slice: x: 4, y: 8, z: 8, core: 2. Of those that a mesh axis runs over, the one named last changes fastest.
Arguments:
- hidden_in: bfloat16 [4096, 2560], P('gx'), may hold values from -48 to 48
- norm_gain: bfloat16 [2560], replicated, may hold values from 0.099609375 to 1.8984375
- router_weight: bfloat16 [2560, 64], replicated, may hold values from -3 to 3
- routes: int32 [4096, 6], P('gx'), may hold values from 0 to 63, as said below
- w_gate_up: bfloat16 [512, 2560, 384], P(('gx', 'gy')), may hold values from -0.125 to 0.125
- w_down: bfloat16 [512, 192, 2560], P(('gx', 'gy')), may hold values from -0.15625 to 0.15625
- final_gain: bfloat16 [2560], replicated, may hold values from 0.099609375 to 1.8984375
- head_weight: bfloat16 [2560, 53248], P('gy', 'gx'), may hold values from -5 to 5
- targets: int32 [4096], replicated, may hold values from 0 to 53247
Outputs:
- logprob: float32 [32, 128], P(None, 'gy')
- entropy: float32 [32, 128], P(None, 'gy')
Inputs may be any that keep to these rules, and one draw needn't show every extreme that they name: `routes`: each row names 6 different experts. Within the 128 rows of one index of gx no expert is named by more than 16 rows, and one expert, the same for every index of gx, is named by exactly 16 rows in each.
All inputs are finite; a program needn't handle non-finite values.
Results may differ from a plain program's by a relative error of at most 0.012.
Values may be sent and summed in bfloat16 or wider, within the bound.
A program may use at most 192 MiB of HBM per device.

v0:
```python
import jax
import jax.numpy as jnp
from jax import lax
from jax.sharding import PartitionSpec as P

SPLITS = 8
NORM_EPSILON = 1e-06


def rms_scale(values, gain_vector):
    widened = values.astype(jnp.float32)
    return (
        widened
        * lax.rsqrt(jnp.mean(widened * widened, -1, keepdims=True) + NORM_EPSILON)
        * gain_vector.astype(jnp.float32)
    )


def finish(peak_value, total_mass, spread, target_logit):
    log_mass = jnp.log(total_mass)
    return (target_logit - peak_value - log_mass, log_mass - spread / total_mass)


def shards(
    hidden_in, norm_gain, router_weight, routes, w_gate_up, w_down, final_gain, head_weight, targets
):
    tok_rows = hidden_in.shape[0]
    group_count = lax.axis_size("gx")
    lane_count = lax.axis_size("gy")
    group_index = lax.axis_index("gx")
    lane_index = lax.axis_index("gy")
    expert_count = router_weight.shape[1]
    held_slices = w_gate_up.shape[0]
    unit_count = w_down.shape[1]
    slot_count = tok_rows // 8
    share_rows = tok_rows // lane_count
    columns = head_weight.shape[1]
    normed = rms_scale(hidden_in, norm_gain).astype(jnp.bfloat16)
    scores = jnp.dot(normed, router_weight, preferred_element_type=jnp.float32)
    chosen = routes[:, :, None] == jnp.arange(expert_count, dtype=jnp.int32)[None, None, :]
    picked = jnp.sum(jnp.where(chosen, scores[:, None, :], 0.0), -1)
    gate_values = jax.nn.softmax(picked, axis=-1).astype(jnp.bfloat16)
    gate_table = jnp.sum(jnp.where(chosen, gate_values.astype(jnp.float32)[:, :, None], 0.0), 1)
    member = jnp.sum(chosen.astype(jnp.int32), 1)
    slot_rank = jnp.cumsum(member, 0) - member
    slot_hit = (member[:, :, None] == 1) & (
        slot_rank[:, :, None] == jnp.arange(slot_count, dtype=jnp.int32)[None, None, :]
    )
    lane_slices = (
        jnp.arange(group_count, dtype=jnp.int32)[:, None] * lane_count + lane_index
    ) * held_slices + jnp.arange(held_slices, dtype=jnp.int32)[None, :]
    owner_expert = lane_slices // SPLITS
    pick_expert = (
        owner_expert[:, :, None] == jnp.arange(expert_count, dtype=jnp.int32)[None, None, :]
    ).astype(jnp.bfloat16)
    dispatch = jnp.einsum(
        "tke,nec->tkcn",
        pick_expert,
        slot_hit.astype(jnp.bfloat16),
        preferred_element_type=jnp.float32,
    ).astype(jnp.bfloat16)
    outgoing = jnp.einsum(
        "tkcn,nd->tkcd", dispatch, normed, preferred_element_type=jnp.float32
    ).astype(jnp.bfloat16)
    expert_gate = jnp.einsum(
        "tke,ne->tkn",
        pick_expert,
        gate_table.astype(jnp.bfloat16),
        preferred_element_type=jnp.float32,
    )
    combine = (dispatch.astype(jnp.float32) * expert_gate[:, :, None, :]).astype(jnp.bfloat16)
    lifted = jnp.einsum(
        "skcd,kdf->skcf",
        lax.all_to_all(outgoing, "gx", split_axis=0, concat_axis=0, tiled=True),
        w_gate_up,
        preferred_element_type=jnp.float32,
    )
    active = (jax.nn.silu(lifted[..., :unit_count]) * lifted[..., unit_count:]).astype(jnp.bfloat16)
    result = jnp.einsum(
        "skcf,kfd->skcd", active, w_down, preferred_element_type=jnp.float32
    ).astype(jnp.bfloat16)
    returned = lax.all_to_all(result, "gx", split_axis=0, concat_axis=0, tiled=True)
    partial_value = jnp.einsum(
        "tkcn,tkcd->nd", combine, returned, preferred_element_type=jnp.float32
    )
    summed = lax.psum_scatter(partial_value, "gy", scatter_dimension=0, tiled=True)
    residual = lax.dynamic_slice_in_dim(hidden_in, lane_index * share_rows, share_rows, 0)
    layer_out = (residual.astype(jnp.float32) + summed).astype(jnp.bfloat16)
    final_states = rms_scale(layer_out, final_gain).astype(jnp.bfloat16)
    gathered = lax.all_gather(final_states, "gx", axis=0, tiled=True)
    target_grid = targets.reshape(group_count, tok_rows)
    logits = jnp.dot(
        gathered,
        lax.all_gather(head_weight, "gy", axis=0, tiled=True),
        preferred_element_type=jnp.float32,
    )
    offset = group_index * columns
    own_targets = lax.dynamic_slice_in_dim(
        target_grid, lane_index * share_rows, share_rows, 1
    ).reshape(group_count * share_rows)
    target_hits = (offset + jnp.arange(columns, dtype=jnp.int32))[None, :] == own_targets[:, None]
    peak_value = lax.pmax(jnp.max(logits, -1), "gx")
    shifted = logits - peak_value[:, None]
    weights = jnp.exp(shifted)
    total_mass, spread, target_logit = lax.psum(
        (
            jnp.sum(weights, -1),
            jnp.sum(weights * shifted, -1),
            jnp.sum(jnp.where(target_hits, logits, 0.0), -1),
        ),
        "gx",
    )
    logprob, entropy = finish(peak_value, total_mass, spread, target_logit)
    return (logprob.reshape(group_count, share_rows), entropy.reshape(group_count, share_rows))


def solution(mesh):
    return jax.shard_map(
        shards,
        mesh=mesh,
        in_specs=(
            P("gx", None),
            P(),
            P(),
            P("gx", None),
            P(("gx", "gy"), None, None),
            P(("gx", "gy"), None, None),
            P(),
            P("gy", "gx"),
            P(),
        ),
        out_specs=(P(None, "gy"), P(None, "gy")),
        check_vma=False,
    )
```

profile of v0, /device:TPU:2, one launch (start us, length us, event | category | flops | bytes accessed | tf_op | source)
XLA Modules:
  0.0 525.7 jit_solution(14808827266614481248)
XLA Ops:
  7.2 0.0 copy-start
  7.2 0.0 copy-start.1
  7.2 0.9 convert_reduce_fusion
  8.1 0.1 copy.35
  8.2 0.7 convert_element_type.89
  8.9 1.3 fusion.8
  10.2 0.2 reduce_window_sum.11
  10.4 0.1 copy.37
  10.4 0.3 convolution_convert_fusion.2
  10.7 0.0 copy-done.1
  10.7 0.9 fusion.1
  11.7 71.8 %all_to_all.10 = bf16[32,1,16,2560]{3,2,1,0:T(8,128)(2,1)S(1)} all-to-all(bf16[32,1,16,2560]{3,2,1,0:T(8,128)(2,1)S(1)} %fusion.1), channel_id=1, replica_groups=mesh['gx'=32,'gy'=16] {'gx'}, dimensions={0} | all-to-all | bytes 5242880 | tf_op jit(solution)/shard_map/all_to_all | solution.py:74
  83.5 0.0 copy-done
  83.5 0.0 copy-start.5
  83.5 1.5 fusion.11
  85.0 0.0 copy-done.5
  85.0 2.4 fusion
  87.5 0.0 copy-start.6
  87.5 5.8 %all-to-all-start.1 = ((bf16[32,1,16,2560]{3,2,1,0:T(8,128)(2,1)}), bf16[32,1,16,2560]{3,2,1,0:T(8,128)(2,1)}, u32[]{:S(2)}, u32[]{:S(2)}) async-start(bf16[32,1,16,2560]{3,2,1,0:T(8,128)(2,1)} %fusion), calls=%async_computation.1 | async-start | bytes 5242880 | tf_op jit(solution)/shard_map/all_to_all | solution.py:82
  93.3 0.0 reduce-scatter.2.cloned.1.call-start
  93.3 0.0 copy-done.6
  93.3 0.4 fusion.26
  93.8 0.0 copy-done.2
  93.9 0.2 fusion.36
  94.1 58.5 %all-to-all-done.1 = bf16[32,1,16,2560]{3,2,1,0:T(8,128)(2,1)} async-done(((bf16[32,1,16,2560]{3,2,1,0:T(8,128)(2,1)}), bf16[32,1,16,2560]{3,2,1,0:T(8,128)(2,1)}, u32[]{:S(2)}, u32[]{:S(2)}) %all-to-all-start.1) | async-done | bytes 2621472 | tf_op jit(solution)/shard_map/all_to_all | solution.py:82
  152.6 4.5 convolution_bitcast_fusion
  157.1 0.0 reduce-scatter.2.cloned.1.call-update
  157.1 0.0 all-gather.3.cloned.1.call-start
  157.2 0.0 copy-done.4
  157.2 62.9 %reduce-scatter.2.cloned.1.call-done = f32[8,2560]{1,0:T(8,128)} async-done(((f32[128,2560]{1,0:T(8,128)}), f32[8,2560]{1,0:T(8,128)}) %reduce-scatter.2.cloned.1.call-update) | async-done | bytes 81936 | tf_op jit(solution)/shard_map/reduce_scatter | solution.py:86
  220.1 1.0 fusion.33
  221.1 0.7 fusion.35
  221.8 0.0 all-gather.3.cloned.1.call-update
  221.8 0.0 all-gather.5.cloned.1.call-start
  221.9 0.7 all-gather.5.cloned.1.call-update
  222.6 0.0 copy-done.3
  222.6 0.1 constant_dynamic-slice_fusion
  222.7 0.1 eq.70
  222.8 79.2 %all-gather.3.cloned.1.call-done = bf16[256,2560]{1,0:T(8,128)(2,1)} async-done(((bf16[8,2560]{1,0:T(8,128)(2,1)}), bf16[256,2560]{1,0:T(8,128)(2,1)}) %all-gather.3.cloned.1.call-update) | async-done | bytes 1310736 | tf_op jit(solution)/shard_map/all_gather | solution.py:90
  301.9 61.2 %all-gather.5.cloned.1.call-done = bf16[2560,1664]{1,0:T(8,128)(2,1)} async-done(((bf16[160,1664]{1,0:T(8,128)(2,1)}), bf16[2560,1664]{1,0:T(8,128)(2,1)}) %all-gather.5.cloned.1.call-update) | async-done | bytes 8519696 | tf_op jit(solution)/shard_map/all_gather | solution.py:94
  363.1 7.6 %fusion.45 = (f32[256]{0:T(256)S(1)}, f32[256,1664]{1,0:T(8,128)}) fusion(bf16[256,2560]{1,0:T(8,128)(2,1)} %all-gather.3.cloned.1.call-done, bf16[2560,1664]{1,0:T(8,128)(2,1)} %all-gather.5.cloned.1.call-done), kind=kOutput, calls=%fused_computation.68 | convolution fusion | flops 2181463808 | bytes 11535360 | tf_op jit(solution)/shard_map/dot_general | solution.py:92
  370.7 70.6 %pmax.7 = f32[256]{0:T(256)S(1)} all-reduce(f32[256]{0:T(256)S(1)} %get-tuple-element.18), channel_id=1, replica_groups=mesh['gx'=32,'gy'=16] {'gx'}, use_global_device_ids=true, to_apply=%region_12.13 | all-reduce | flops 256 | bytes 2048 | tf_op jit(solution)/shard_map/pmax | solution.py:102
  441.4 2.1 fusion.7
  443.5 74.1 %all-reduce = (f32[256]{0:T(256)S(1)}, f32[256]{0:T(256)S(1)}, f32[256]{0:T(256)S(1)}) all-reduce(f32[256]{0:T(256)S(1)} %get-tuple-element.10, f32[256]{0:T(256)S(1)} %get-tuple-element.9, f32[256]{0:T(256)S(1)} %get-tuple-element.8), channel_id=1, replica_groups=mesh['gx'=32,'gy'=16] {'gx'}, use_global_device_ids=true, to_apply=%region_10.11 | all-reduce | flops 768 | bytes 6144 | tf_op jit(solution)/shard_map/psum | solution.py:105
  517.6 0.1 reshape.187
  517.7 0.7 copy.42
  518.4 0.1 reshape.188
  518.5 0.7 copy.43
  (16 shorter events, 0.2 us)
Async XLA Ops:
  7.2 76.3 %copy-start = (bf16[1,2560,384]{2,1,0:T(8,128)(2,1)S(1)}, bf16[1,2560,384]{2,1,0:T(8,128)(2,1)}, u32[]{:S(2)}) copy-start(bf16[1,2560,384]{2,1,0:T(8,128)(2,1)} %param.13) | copy-start | bytes 5898244
  7.2 3.5 copy-start.1
  83.5 1.5 copy-start.5
  87.5 5.8 %copy-start.6 = (bf16[2560,64]{0,1:T(8,128)(2,1)S(1)}, bf16[2560,64]{0,1:T(8,128)(2,1)}, u32[]{:S(2)}) copy-start(bf16[2560,64]{0,1:T(8,128)(2,1)} %param.11) | copy-start | bytes 983044
  87.5 6.3 %copy-start.2 = (s32[128,6]{0,1:T(8,128)S(1)}, s32[128,6]{0,1:T(8,128)}, u32[]{:S(2)}) copy-start(s32[128,6]{0,1:T(8,128)} %param.12) | copy-start | bytes 9220
  87.5 65.1 %all-to-all-start.1 = ((bf16[32,1,16,2560]{3,2,1,0:T(8,128)(2,1)}), bf16[32,1,16,2560]{3,2,1,0:T(8,128)(2,1)}, u32[]{:S(2)}, u32[]{:S(2)}) async-start(bf16[32,1,16,2560]{3,2,1,0:T(8,128)(2,1)} %fusion), calls=%async_computation.1 | async-start | bytes 5242880 | tf_op jit(solution)/shard_map/all_to_all | solution.py:82
  93.3 126.8 %reduce-scatter.2.cloned.1.call-start = ((), (), s32[]{:S(2)}) async-start(), calls=%async_computation.3 | async-start | bytes 1392640 | tf_op jit(solution)/shard_map/reduce_scatter | solution.py:86
  94.1 63.1 %copy-start.4 = (bf16[2560]{0:T(1024)(128)(2,1)S(1)}, bf16[2560]{0:T(1024)(128)(2,1)}, u32[]{:S(2)}) copy-start(bf16[2560]{0:T(1024)(128)(2,1)} %param.15) | copy-start | bytes 15364
  157.1 65.5 %copy-start.3 = (s32[4096]{0:T(1024)S(1)}, s32[4096]{0:T(1024)}, u32[]{:S(2)}) copy-start(s32[4096]{0:T(1024)} %param.17) | copy-start | bytes 49156
  157.1 144.8 %all-gather.3.cloned.1.call-start = ((), (), s32[]{:S(2)}) async-start(), calls=%async_computation.4 | async-start | bytes 1351680 | tf_op jit(solution)/shard_map/all_gather | solution.py:90
  221.8 141.3 %all-gather.5.cloned.1.call-start = ((), (), s32[]{:S(2)}) async-start(), calls=%async_computation.5 | async-start | bytes 9052160 | tf_op jit(solution)/shard_map/all_gather | solution.py:94
Sparse Core Ops, SparseCore 0:
  157.2 62.7 reduce-scatter.1
  223.2 78.6 all-gather.2
  304.1 59.0 all-gather.4
where the time goes:
time: 526 us
  waiting for transfers between devices  262 us (50%)
  blocking collectives  217 us (41%)
  matrix products  17.9 us (3%)
  between operations  13.9 us (3%)
  other arithmetic  7.05 us (1%)
  starting transfers between devices  5.9 us (1%)
    all_gather x1, waiting for transfers between devices, shards(): gathered = lax.all_gather(final_states, 'gx', axis=0, tiled=True)  79.2 us
    psum x1, blocking collectives, shards(): lax.psum((jnp.sum(weights, -1), jnp.sum(weights * shifted, -1), jnp.sum(j...  74.1 us
    all_to_all x1, blocking collectives, shards(): lax.all_to_all(outgoing, 'gx', split_axis=0, concat_axis=0, tiled=True)  71.8 us
    pmax x1, blocking collectives, shards(): peak_value = lax.pmax(jnp.max(logits, -1), 'gx')  70.6 us
    reduce_scatter x1, waiting for transfers between devices, shards(): lax.psum_scatter(partial_value, 'gy', scatter_dimension=0, tiled=True)  62.9 us
    all_gather x1, waiting for transfers between devices, shards(): lax.all_gather(head_weight, 'gy', axis=0, tiled=True)  61.2 us
    all_to_all x1, waiting for transfers between devices, shards(): lax.all_to_all(result, 'gx', split_axis=0, concat_axis=0, tiled=True)  58.5 us
  transfers between devices with their start and end apart: 4, of which 4 were waited for; matrix products, arithmetic and copies ran while one was open for 0% of the time, Pallas kernels for 0%

commit v1 on v0

--- a/solution.py
+++ b/solution.py
@@ -5,6 +5,19 @@
 
 SPLITS = 8
 NORM_EPSILON = 1e-06
+
+
+def ring_gather(shard, axis, dim):
+    ways = lax.axis_size(axis)
+    up = [(d, (d + 1) % ways) for d in range(ways)]
+    down = [(d, (d - 1) % ways) for d in range(ways)]
+    earlier, later = ([shard], [shard])
+    for _ in range(ways // 2):
+        earlier.append(lax.ppermute(earlier[-1], axis, up))
+    for _ in range((ways - 1) // 2):
+        later.append(lax.ppermute(later[-1], axis, down))
+    line = jnp.concatenate([*earlier[::-1], *later[1:]], axis=dim)
+    return jnp.roll(line, (lax.axis_index(axis) - ways // 2) * shard.shape[dim], axis=dim)
 
 
 def rms_scale(values, gain_vector):
@@ -90,9 +103,7 @@
     gathered = lax.all_gather(final_states, "gx", axis=0, tiled=True)
     target_grid = targets.reshape(group_count, tok_rows)
     logits = jnp.dot(
-        gathered,
-        lax.all_gather(head_weight, "gy", axis=0, tiled=True),
-        preferred_element_type=jnp.float32,
+        gathered, ring_gather(head_weight, "gy", 0), preferred_element_type=jnp.float32
     )
     offset = group_index * columns
     own_targets = lax.dynamic_slice_in_dim(

time: 526 us -> 474 us (0.901)
  waiting for transfers between devices: 262 us -> 177 us
  blocking collectives: 217 us -> 143 us
  local copies, waits for them, and re-layouts: 1.86 us -> 61.7 us
  starting transfers between devices: 5.9 us -> 44.4 us
  matrix products: 17.9 us -> 24.4 us
    all_to_all x1 -> x0, blocking collectives: 71.8 us -> none  [shards(): lax.all_to_all(outgoing, 'gx', split_axis=0, concat_axis=0, tiled=True)]
    all_gather x1 -> x0, waiting for transfers between devices: 61.2 us -> none  [shards(): lax.all_gather(head_weight, 'gy', axis=0, tiled=True)]
    all_to_all x1, waiting for transfers between devices: 58.5 us -> 0.01 us  [shards(): lax.all_to_all(result, 'gx', split_axis=0, concat_axis=0, tiled=True)]
    unnamed x16 -> x51, local copies, waits for them, and re-layouts: 1.38 us -> 59.4 us
    ppermute x0 -> x15, waiting for transfers between devices: none -> 55.6 us  [the longest x8 29.1 us: ring_gather(): earlier.append(lax.ppermute(earlier[-1], axis, up))]
    ppermute x0 -> x15, starting transfers between devices: none -> 26.7 us  [the longest x7 26.7 us: ring_gather(): later.append(lax.ppermute(later[-1], axis, down))]
    reduce_scatter x1, waiting for transfers between devices: 62.9 us -> 37.6 us  [shards(): lax.psum_scatter(partial_value, 'gy', scatter_dimension=0, tiled=True)]
    all_to_all x0 -> x1, waiting for transfers between devices: none -> 23.5 us  [shards(): lax.all_to_all(outgoing, 'gx', split_axis=0, concat_axis=0, tiled=True)]
  transfers between devices with their start and end apart: 4 -> 19, of which waited for: 4 -> 10; matrix products, arithmetic and copies ran while one was open for 0% -> 15% of each run, Pallas kernels for 0% -> 0%
where the time goes in v1:
time: 474 us; the launch traced here: 472 us
  waiting for transfers between devices  177 us (37%)
  blocking collectives  143 us (30%)
  local copies, waits for them, and re-layouts  61.7 us (13%)
  starting transfers between devices  44.4 us (9%)
  matrix products  24.4 us (5%)
  between operations  14.3 us (3%)
  other arithmetic  7.03 us (1%)
    psum x1, blocking collectives, shards(): lax.psum((jnp.sum(weights, -1), jnp.sum(weights * shifted, -1), jnp.sum(j...  72.1 us
    pmax x1, blocking collectives, shards(): peak_value = lax.pmax(jnp.max(logits, -1), 'gx')  71.3 us
    all_gather x1, waiting for transfers between devices, shards(): gathered = lax.all_gather(final_states, 'gx', axis=0, tiled=True)  60.3 us
    unnamed x51, local copies, waits for them, and re-layouts  59.4 us
    reduce_scatter x1, waiting for transfers between devices, shards(): lax.psum_scatter(partial_value, 'gy', scatter_dimension=0, tiled=True)  37.6 us
    ppermute x8, waiting for transfers between devices, ring_gather(): earlier.append(lax.ppermute(earlier[-1], axis, up))  29.1 us
    ppermute x7, starting transfers between devices, ring_gather(): later.append(lax.ppermute(later[-1], axis, down))  26.7 us
    ppermute x7, waiting for transfers between devices, ring_gather(): later.append(lax.ppermute(later[-1], axis, down))  26.4 us
  transfers between devices with their start and end apart: 19, of which 10 were waited for; matrix products, arithmetic and copies ran while one was open for 15% of the time, Pallas kernels for 0%

profile of v1, /device:TPU:2, one launch (start us, length us, event | category | flops | bytes accessed | tf_op | source)
XLA Modules:
  0.0 472.2 jit_solution(8768627438559697953)
XLA Ops:
  10.7 3.6 fusion.3
  14.3 10.3 %all-to-all-start = ((bf16[32,1,16,2560]{3,2,1,0:T(8,128)(2,1)}), bf16[32,1,16,2560]{3,2,1,0:T(8,128)(2,1)}, u32[]{:S(2)}, u32[]{:S(2)}) async-start(bf16[32,1,16,2560]{3,2,1,0:T(8,128)(2,1)} %fusion.3), calls=%async_computation | async-start | bytes 5242880 | tf_op jit(solution)/shard_map/all_to_all | solution.py:87
  24.6 15.1 %collective-permute-done = bf16[160,1664]{1,0:T(8,128)(2,1)S(1)} collective-permute-done((bf16[160,1664]{1,0:T(8,128)(2,1)}, bf16[160,1664]{1,0:T(8,128)(2,1)S(1)}, u32[]{:S(2)}, u32[]{:S(2)}) %collective-permute-start) | collective-permute-done | bytes 532512 | tf_op jit(solution)/shard_map/ppermute | solution.py:16
  40.6 3.0 collective-permute-start.8
  43.5 6.9 %collective-permute-done.1 = bf16[160,1664]{1,0:T(8,128)(2,1)S(1)} collective-permute-done((bf16[160,1664]{1,0:T(8,128)(2,1)S(1)}, bf16[160,1664]{1,0:T(8,128)(2,1)S(1)}, u32[]{:S(2)}, u32[]{:S(2)}) %collective-permute-start.1) | collective-permute-done | bytes 532512 | tf_op jit(solution)/shard_map/ppermute | solution.py:16
  51.3 3.0 collective-permute-start.9
  54.2 7.0 %collective-permute-done.2 = bf16[160,1664]{1,0:T(8,128)(2,1)} collective-permute-done((bf16[160,1664]{1,0:T(8,128)(2,1)S(1)}, bf16[160,1664]{1,0:T(8,128)(2,1)}, u32[]{:S(2)}, u32[]{:S(2)}) %collective-permute-start.2) | collective-permute-done | bytes 532512 | tf_op jit(solution)/shard_map/ppermute | solution.py:16
  61.3 23.5 %all-to-all-done = bf16[32,1,16,2560]{3,2,1,0:T(8,128)(2,1)} async-done(((bf16[32,1,16,2560]{3,2,1,0:T(8,128)(2,1)}), bf16[32,1,16,2560]{3,2,1,0:T(8,128)(2,1)}, u32[]{:S(2)}, u32[]{:S(2)}) %all-to-all-start) | async-done | bytes 2621472 | tf_op jit(solution)/shard_map/all_to_all | solution.py:87
  84.7 3.2 fusion.13
  88.0 3.6 fusion.2
  91.6 7.3 %all-to-all-start.1 = ((bf16[32,1,16,2560]{3,2,1,0:T(8,128)(2,1)}), bf16[32,1,16,2560]{3,2,1,0:T(8,128)(2,1)}, u32[]{:S(2)}, u32[]{:S(2)}) async-start(bf16[32,1,16,2560]{3,2,1,0:T(8,128)(2,1)} %fusion.2), calls=%async_computation.1 | async-start | bytes 5242880 | tf_op jit(solution)/shard_map/all_to_all | solution.py:95
  99.0 7.1 %collective-permute-start.10 = (bf16[160,1664]{1,0:T(8,128)(2,1)}, bf16[160,1664]{1,0:T(8,128)(2,1)}, u32[]{:S(2)}, u32[]{:S(2)}) collective-permute-start(bf16[160,1664]{1,0:T(8,128)(2,1)} %collective-permute-done.9), channel_id=1, source_target_pairs={{0,15},{1,0},{2,1},{3,2},{4,3},{5,4},{6,5},{7,6},{8,7},{9,8},{10,9... | collective-permute-start | bytes 1597448 | tf_op jit(solution)/shard_map/ppermute | solution.py:18
  106.1 7.1 %collective-permute-done.10 = bf16[160,1664]{1,0:T(8,128)(2,1)} collective-permute-done((bf16[160,1664]{1,0:T(8,128)(2,1)}, bf16[160,1664]{1,0:T(8,128)(2,1)}, u32[]{:S(2)}, u32[]{:S(2)}) %collective-permute-start.10) | collective-permute-done | bytes 532512 | tf_op jit(solution)/shard_map/ppermute | solution.py:18
  113.2 3.4 collective-permute-start.11
  116.8 6.9 %collective-permute-done.11 = bf16[160,1664]{1,0:T(8,128)(2,1)} collective-permute-done((bf16[160,1664]{1,0:T(8,128)(2,1)}, bf16[160,1664]{1,0:T(8,128)(2,1)}, u32[]{:S(2)}, u32[]{:S(2)}) %collective-permute-start.11) | collective-permute-done | bytes 532512 | tf_op jit(solution)/shard_map/ppermute | solution.py:18
  123.7 3.4 collective-permute-start.12
  128.6 5.6 %collective-permute-done.12 = bf16[160,1664]{1,0:T(8,128)(2,1)} collective-permute-done((bf16[160,1664]{1,0:T(8,128)(2,1)}, bf16[160,1664]{1,0:T(8,128)(2,1)}, u32[]{:S(2)}, u32[]{:S(2)}) %collective-permute-start.12) | collective-permute-done | bytes 532512 | tf_op jit(solution)/shard_map/ppermute | solution.py:18
  134.2 3.4 collective-permute-start.13
  137.9 6.9 %collective-permute-done.13 = bf16[160,1664]{1,0:T(8,128)(2,1)} collective-permute-done((bf16[160,1664]{1,0:T(8,128)(2,1)}, bf16[160,1664]{1,0:T(8,128)(2,1)}, u32[]{:S(2)}, u32[]{:S(2)}) %collective-permute-start.13) | collective-permute-done | bytes 532512 | tf_op jit(solution)/shard_map/ppermute | solution.py:18
  144.8 3.4 collective-permute-start.14
  149.9 1.9 constant_dynamic-update-slice_fusion.30
  151.8 1.9 constant_dynamic-update-slice_fusion.29
  153.7 1.9 constant_dynamic-update-slice_fusion.28
  157.4 1.9 constant_dynamic-update-slice_fusion.26
  163.9 1.9 constant_dynamic-update-slice_fusion.22
  165.8 4.5 convolution_bitcast_fusion
  170.4 1.9 constant_dynamic-update-slice_fusion.21
  174.2 1.9 constant_dynamic-update-slice_fusion.19
  176.1 1.9 constant_dynamic-update-slice_fusion.18
  179.8 1.9 constant_dynamic-update-slice_fusion.16
  181.7 1.9 constant_dynamic-update-slice_fusion.15
  183.7 1.9 constant_dynamic-update-slice_fusion.14
  185.6 1.9 constant_dynamic-update-slice_fusion.13
  189.4 1.9 constant_dynamic-update-slice_fusion.11
  191.3 37.6 %reduce-scatter.2.cloned.1.call-done = f32[8,2560]{1,0:T(8,128)} async-done(((f32[128,2560]{1,0:T(8,128)}), f32[8,2560]{1,0:T(8,128)}) %reduce-scatter.2.cloned.1.call-update) | async-done | bytes 81936 | tf_op jit(solution)/shard_map/reduce_scatter | solution.py:99
  230.6 1.9 constant_dynamic-update-slice_fusion.10
  234.3 1.9 constant_dynamic-update-slice_fusion.8
  237.1 1.9 constant_dynamic-update-slice_fusion.6
  239.0 1.9 constant_dynamic-update-slice_fusion.5
  242.7 1.9 constant_dynamic-update-slice_fusion.3
  244.6 1.9 constant_dynamic-update-slice_fusion.2
  246.5 1.9 constant_dynamic-update-slice_fusion.1
  248.4 1.9 constant_dynamic-update-slice_fusion
  250.3 60.3 %all-gather.2.cloned.1.call-done = bf16[256,2560]{1,0:T(8,128)(2,1)} async-done(((bf16[8,2560]{1,0:T(8,128)(2,1)}), bf16[256,2560]{1,0:T(8,128)(2,1)}) %all-gather.2.cloned.1.call-update) | async-done | bytes 1310736 | tf_op jit(solution)/shard_map/all_gather | solution.py:103
  310.7 7.6 %fusion.48 = (f32[256]{0:T(256)S(1)}, f32[256,1664]{1,0:T(8,128)}) fusion(bf16[256,2560]{1,0:T(8,128)(2,1)} %all-gather.2.cloned.1.call-done, bf16[5120,1664]{1,0:T(8,128)(2,1)} %constant_dynamic-update-slice_fusion, s32[]{:T(128)S(6)} %select_n.45), kind=kOutput, calls=%fused_computation.103 | convolution fusion | flops 2181463808 | bytes 11535364 | tf_op jit(solution)/shard_map/dot_general | solution.py:105
  318.3 71.3 %pmax.7 = f32[256]{0:T(256)S(1)} all-reduce(f32[256]{0:T(256)S(1)} %get-tuple-element.18), channel_id=1, replica_groups=mesh['gx'=32,'gy'=16] {'gx'}, use_global_device_ids=true, to_apply=%region_12.13 | all-reduce | flops 256 | bytes 2048 | tf_op jit(solution)/shard_map/pmax | solution.py:113
  389.6 2.1 fusion.9
  391.8 72.1 %all-reduce = (f32[256]{0:T(256)S(1)}, f32[256]{0:T(256)S(1)}, f32[256]{0:T(256)S(1)}) all-reduce(f32[256]{0:T(256)S(1)} %get-tuple-element.10, f32[256]{0:T(256)S(1)} %get-tuple-element.9, f32[256]{0:T(256)S(1)} %get-tuple-element.8), channel_id=1, replica_groups=mesh['gx'=32,'gy'=16] {'gx'}, use_global_device_ids=true, to_apply=%region_10.11 | all-reduce | flops 768 | bytes 6144 | tf_op jit(solution)/shard_map/psum | solution.py:116
  (80 shorter events, 28.8 us)
Async XLA Ops:
  7.2 77.6 %copy-start = (bf16[1,2560,384]{2,1,0:T(8,128)(2,1)S(1)}, bf16[1,2560,384]{2,1,0:T(8,128)(2,1)}, u32[]{:S(2)}) copy-start(bf16[1,2560,384]{2,1,0:T(8,128)(2,1)} %param.13) | copy-start | bytes 5898244
  7.2 120.0 %copy-start.1 = (bf16[128,2560]{1,0:T(8,128)(2,1)S(1)}, bf16[128,2560]{1,0:T(8,128)(2,1)}, u32[]{:S(2)}) copy-start(bf16[128,2560]{1,0:T(8,128)(2,1)} %param.9) | copy-start | bytes 1966084
  7.2 109.4 %copy-start.8 = (bf16[2560]{0:T(1024)(128)(2,1)S(1)}, bf16[2560]{0:T(1024)(128)(2,1)}, u32[]{:S(2)}) copy-start(bf16[2560]{0:T(1024)(128)(2,1)} %param.15) | copy-start | bytes 15364
  7.2 109.5 %copy-start.7 = (s32[4096]{0:T(1024)S(1)}, s32[4096]{0:T(1024)}, u32[]{:S(2)}) copy-start(s32[4096]{0:T(1024)} %param.17) | copy-start | bytes 49156
  10.2 118.3 %copy-start.6 = (s32[128,6]{0,1:T(8,128)S(1)}, s32[128,6]{0,1:T(8,128)}, u32[]{:S(2)}) copy-start(s32[128,6]{0,1:T(8,128)} %param.12) | copy-start | bytes 9220
  14.3 70.4 %all-to-all-start = ((bf16[32,1,16,2560]{3,2,1,0:T(8,128)(2,1)}), bf16[32,1,16,2560]{3,2,1,0:T(8,128)(2,1)}, u32[]{:S(2)}, u32[]{:S(2)}) async-start(bf16[32,1,16,2560]{3,2,1,0:T(8,128)(2,1)} %fusion.3), calls=%async_computation | async-start | bytes 5242880 | tf_op jit(solution)/shard_map/all_to_all | solution.py:87
  24.6 138.4 %copy-start.2 = (bf16[160,1664]{1,0:T(8,128)(2,1)S(1)}, bf16[160,1664]{1,0:T(8,128)(2,1)}, u32[]{:S(2)}) copy-start(bf16[160,1664]{1,0:T(8,128)(2,1)} %param.16) | copy-start | bytes 1597444
  24.6 15.1 %collective-permute-start = (bf16[160,1664]{1,0:T(8,128)(2,1)}, bf16[160,1664]{1,0:T(8,128)(2,1)S(1)}, u32[]{:S(2)}, u32[]{:S(2)}) collective-permute-start(bf16[160,1664]{1,0:T(8,128)(2,1)} %param.16), channel_id=1, source_target_pairs={{0,1},{1,2},{2,3},{3,4},{4,5},{5,6},{6,7},{7,8},{8,9},{9,10},{10,1... | collective-permute-start | bytes 1597448 | tf_op jit(solution)/shard_map/ppermute | solution.py:16
  39.8 0.8 copy-start.3
  40.6 9.9 %collective-permute-start.1 = (bf16[160,1664]{1,0:T(8,128)(2,1)S(1)}, bf16[160,1664]{1,0:T(8,128)(2,1)S(1)}, u32[]{:S(2)}, u32[]{:S(2)}) collective-permute-start(bf16[160,1664]{1,0:T(8,128)(2,1)S(1)} %collective-permute-done), channel_id=1, source_target_pairs={{0,1},{1,2},{2,3},{3,4},{4,5},{5,6},{6,7},{7,8},{8,9},{9,10},{10,1... | collective-permute-start | bytes 1597448 | tf_op jit(solution)/shard_map/ppermute | solution.py:16
  40.6 10.7 %collective-permute-start.8 = (bf16[160,1664]{1,0:T(8,128)(2,1)}, bf16[160,1664]{1,0:T(8,128)(2,1)}, u32[]{:S(2)}, u32[]{:S(2)}) collective-permute-start(bf16[160,1664]{1,0:T(8,128)(2,1)} %param.16), channel_id=1, source_target_pairs={{0,15},{1,0},{2,1},{3,2},{4,3},{5,4},{6,5},{7,6},{8,7},{9,8},{10,9... | collective-permute-start | bytes 1597448 | tf_op jit(solution)/shard_map/ppermute | solution.py:18
  50.5 0.8 copy-start.4
  51.3 10.0 %collective-permute-start.2 = (bf16[160,1664]{1,0:T(8,128)(2,1)S(1)}, bf16[160,1664]{1,0:T(8,128)(2,1)}, u32[]{:S(2)}, u32[]{:S(2)}) collective-permute-start(bf16[160,1664]{1,0:T(8,128)(2,1)S(1)} %collective-permute-done.1), channel_id=1, source_target_pairs={{0,1},{1,2},{2,3},{3,4},{4,5},{5,6},{6,7},{7,8},{8,9},{9,10},{10,1... | collective-permute-start | bytes 1597448 | tf_op jit(solution)/shard_map/ppermute | solution.py:16
  51.3 47.7 %collective-permute-start.9 = (bf16[160,1664]{1,0:T(8,128)(2,1)}, bf16[160,1664]{1,0:T(8,128)(2,1)}, u32[]{:S(2)}, u32[]{:S(2)}) collective-permute-start(bf16[160,1664]{1,0:T(8,128)(2,1)} %collective-permute-done.8), channel_id=1, source_target_pairs={{0,15},{1,0},{2,1},{3,2},{4,3},{5,4},{6,5},{7,6},{8,7},{9,8},{10,9... | collective-permute-start | bytes 1597448 | tf_op jit(solution)/shard_map/ppermute | solution.py:18
  61.3 44.8 %collective-permute-start.3 = (bf16[160,1664]{1,0:T(8,128)(2,1)}, bf16[160,1664]{1,0:T(8,128)(2,1)}, u32[]{:S(2)}, u32[]{:S(2)}) collective-permute-start(bf16[160,1664]{1,0:T(8,128)(2,1)} %collective-permute-done.2), channel_id=1, source_target_pairs={{0,1},{1,2},{2,3},{3,4},{4,5},{5,6},{6,7},{7,8},{8,9},{9,10},{10,1... | collective-permute-start | bytes 1597448 | tf_op jit(solution)/shard_map/ppermute | solution.py:16
  91.6 74.2 %all-to-all-start.1 = ((bf16[32,1,16,2560]{3,2,1,0:T(8,128)(2,1)}), bf16[32,1,16,2560]{3,2,1,0:T(8,128)(2,1)}, u32[]{:S(2)}, u32[]{:S(2)}) async-start(bf16[32,1,16,2560]{3,2,1,0:T(8,128)(2,1)} %fusion.2), calls=%async_computation.1 | async-start | bytes 5242880 | tf_op jit(solution)/shard_map/all_to_all | solution.py:95
  98.9 129.9 %reduce-scatter.2.cloned.1.call-start = ((), (), s32[]{:S(2)}) async-start(), calls=%async_computation.3 | async-start | bytes 1392640 | tf_op jit(solution)/shard_map/reduce_scatter | solution.py:99
  99.0 14.2 %collective-permute-start.10 = (bf16[160,1664]{1,0:T(8,128)(2,1)}, bf16[160,1664]{1,0:T(8,128)(2,1)}, u32[]{:S(2)}, u32[]{:S(2)}) collective-permute-start(bf16[160,1664]{1,0:T(8,128)(2,1)} %collective-permute-done.9), channel_id=1, source_target_pairs={{0,15},{1,0},{2,1},{3,2},{4,3},{5,4},{6,5},{7,6},{8,7},{9,8},{10,9... | collective-permute-start | bytes 1597448 | tf_op jit(solution)/shard_map/ppermute | solution.py:18
  106.1 10.5 %collective-permute-start.4 = (bf16[160,1664]{1,0:T(8,128)(2,1)}, bf16[160,1664]{1,0:T(8,128)(2,1)}, u32[]{:S(2)}, u32[]{:S(2)}) collective-permute-start(bf16[160,1664]{1,0:T(8,128)(2,1)} %collective-permute-done.3), channel_id=1, source_target_pairs={{0,1},{1,2},{2,3},{3,4},{4,5},{5,6},{6,7},{7,8},{8,9},{9,10},{10,1... | collective-permute-start | bytes 1597448 | tf_op jit(solution)/shard_map/ppermute | solution.py:16
  113.2 10.5 %collective-permute-start.11 = (bf16[160,1664]{1,0:T(8,128)(2,1)}, bf16[160,1664]{1,0:T(8,128)(2,1)}, u32[]{:S(2)}, u32[]{:S(2)}) collective-permute-start(bf16[160,1664]{1,0:T(8,128)(2,1)} %collective-permute-done.10), channel_id=1, source_target_pairs={{0,15},{1,0},{2,1},{3,2},{4,3},{5,4},{6,5},{7,6},{8,7},{9,8},{10,9... | collective-permute-start | bytes 1597448 | tf_op jit(solution)/shard_map/ppermute | solution.py:18
  116.6 10.5 %collective-permute-start.5 = (bf16[160,1664]{1,0:T(8,128)(2,1)}, bf16[160,1664]{1,0:T(8,128)(2,1)}, u32[]{:S(2)}, u32[]{:S(2)}) collective-permute-start(bf16[160,1664]{1,0:T(8,128)(2,1)} %collective-permute-done.4), channel_id=1, source_target_pairs={{0,1},{1,2},{2,3},{3,4},{4,5},{5,6},{6,7},{7,8},{8,9},{9,10},{10,1... | collective-permute-start | bytes 1597448 | tf_op jit(solution)/shard_map/ppermute | solution.py:16
  123.7 10.5 %collective-permute-start.12 = (bf16[160,1664]{1,0:T(8,128)(2,1)}, bf16[160,1664]{1,0:T(8,128)(2,1)}, u32[]{:S(2)}, u32[]{:S(2)}) collective-permute-start(bf16[160,1664]{1,0:T(8,128)(2,1)} %collective-permute-done.11), channel_id=1, source_target_pairs={{0,15},{1,0},{2,1},{3,2},{4,3},{5,4},{6,5},{7,6},{8,7},{9,8},{10,9... | collective-permute-start | bytes 1597448 | tf_op jit(solution)/shard_map/ppermute | solution.py:18
  127.1 10.5 %collective-permute-start.6 = (bf16[160,1664]{1,0:T(8,128)(2,1)}, bf16[160,1664]{1,0:T(8,128)(2,1)}, u32[]{:S(2)}, u32[]{:S(2)}) collective-permute-start(bf16[160,1664]{1,0:T(8,128)(2,1)} %collective-permute-done.5), channel_id=1, source_target_pairs={{0,1},{1,2},{2,3},{3,4},{4,5},{5,6},{6,7},{7,8},{8,9},{9,10},{10,1... | collective-permute-start | bytes 1597448 | tf_op jit(solution)/shard_map/ppermute | solution.py:16
  134.2 10.5 %collective-permute-start.13 = (bf16[160,1664]{1,0:T(8,128)(2,1)}, bf16[160,1664]{1,0:T(8,128)(2,1)}, u32[]{:S(2)}, u32[]{:S(2)}) collective-permute-start(bf16[160,1664]{1,0:T(8,128)(2,1)} %collective-permute-done.12), channel_id=1, source_target_pairs={{0,15},{1,0},{2,1},{3,2},{4,3},{5,4},{6,5},{7,6},{8,7},{9,8},{10,9... | collective-permute-start | bytes 1597448 | tf_op jit(solution)/shard_map/ppermute | solution.py:18
  137.7 10.5 %collective-permute-start.7 = (bf16[160,1664]{1,0:T(8,128)(2,1)}, bf16[160,1664]{1,0:T(8,128)(2,1)S(1)}, u32[]{:S(2)}, u32[]{:S(2)}) collective-permute-start(bf16[160,1664]{1,0:T(8,128)(2,1)} %collective-permute-done.6), channel_id=1, source_target_pairs={{0,1},{1,2},{2,3},{3,4},{4,5},{5,6},{6,7},{7,8},{8,9},{9,10},{10,1... | collective-permute-start | bytes 1597448 | tf_op jit(solution)/shard_map/ppermute | solution.py:16
  144.8 35.1 %collective-permute-start.14 = (bf16[160,1664]{1,0:T(8,128)(2,1)}, bf16[160,1664]{1,0:T(8,128)(2,1)}, u32[]{:S(2)}, u32[]{:S(2)}) collective-permute-start(bf16[160,1664]{1,0:T(8,128)(2,1)} %collective-permute-done.13), channel_id=1, source_target_pairs={{0,15},{1,0},{2,1},{3,2},{4,3},{5,4},{6,5},{7,6},{8,7},{9,8},{10,9... | collective-permute-start | bytes 1597448 | tf_op jit(solution)/shard_map/ppermute | solution.py:18
  148.2 0.9 copy-start.5
  170.3 140.4 %all-gather.2.cloned.1.call-start = ((), (), s32[]{:S(2)}) async-start(), calls=%async_computation.4 | async-start | bytes 1351680 | tf_op jit(solution)/shard_map/all_gather | solution.py:103
Sparse Core Ops, SparseCore 0:
  170.4 58.3 reduce-scatter.1
  232.0 78.6 all-gather.1
